TPU v7x, 512 devices: a whole 4x8x8 slice. The times are simulated.
512 devices in a mesh: leaf: 128 (over z, y, core), list: 4 (over x).
Axes of the slice: x: 4, y: 8, z: 8, core: 2. Of those that a mesh axis runs over, the one named last changes fastest.
Arguments:
- points: bfloat16 [32, 524288], P(None, 'leaf')
- charges: bfloat16 [32, 524288], P(None, 'leaf'), may hold values from -0.59765625 to 0.59765625
- leaf_ids: int32 [2048, 128], P('leaf'), may hold values from 0 to 255, as said below
- inner_ids: int32 [1920, 128], P('leaf'), may hold values from 0 to 255, as said below
- upper_ids_first: int32 [64, 128], replicated, may hold values from 0 to 255, as said below
- upper_ids_second: int32 [32, 128], replicated, may hold values from 0 to 255, as said below
- upper_ids_third: int32 [16, 128], replicated, may hold values from 0 to 255, as said below
- leaf_maps: bfloat16 [2048, 128, 256], P('leaf'), may hold values from -0.375 to 0.375
- inner_maps: bfloat16 [1920, 128, 256], P('leaf'), may hold values from -0.4375 to 0.4375
- upper_maps_first: bfloat16 [8192, 256], P('leaf'), may hold values from -0.4375 to 0.4375
- upper_maps_second: bfloat16 [4096, 256], P('leaf'), may hold values from -0.4375 to 0.4375
- upper_maps_third: bfloat16 [2048, 256], P('leaf'), may hold values from -0.4375 to 0.4375
- near_lists: int32 [2048, 32], P('leaf', 'list'), may hold values from -1 to 2047, as said below
- far_inner: int32 [3968, 32], P('leaf', 'list'), may hold values from 0 to 2047, as said below
- far_upper_first: int32 [64, 32], P(None, 'list'), may hold values from 0 to 63
- far_upper_second: int32 [32, 32], P(None, 'list'), may hold values from 0 to 31
- far_upper_third: int32 [16, 32], P(None, 'list'), may hold values from 0 to 15
Outputs:
- potentials: float32 [32, 524288], P(None, ('leaf', 'list'))
Inputs may be any that keep to these rules, and one draw needn't show every extreme that they name: `leaf_ids`: each row holds 128 distinct columns of its leaf. `inner_ids`: each row holds 128 distinct columns of its node's 2 * 128 child skeleton columns. `upper_ids_first`: each row holds 128 distinct columns of its node's 2 * 128 child skeleton columns. `upper_ids_second`: each row holds 128 distinct columns of its node's 2 * 128 child skeleton columns. `upper_ids_third`: each row holds 128 distinct columns of its node's 2 * 128 child skeleton columns. `near_lists`: each row starts with one or more leaf numbers and is -1 after them; some row has 32 leaf numbers. A leaf number s in row i satisfies |s // 16 - i // 16| <= 1. `far_inner`: an entry s of node i at level l satisfies |s // (16 >> l) - i // (16 >> l)| <= 1, both numbered within level l.
All inputs are finite; a program needn't handle non-finite values.
Results may differ from a plain program's by a relative error of at most 0.01.
Values may be sent and summed in bfloat16 or wider, within the bound.
A program may use at most 128 MiB of HBM per device.

v0:
```python
import jax
import jax.numpy as jnp
from jax import lax
from jax.sharding import PartitionSpec as P

pair_block = 16


def extended_2(cells, sides, width):
    for axis, dim in sides:
        count = lax.axis_size(axis)
        ends = count - 1
        head = lax.slice_in_dim(cells, 0, width, axis=dim)
        tail = lax.slice_in_dim(cells, cells.shape[dim] - width, cells.shape[dim], axis=dim)
        cells = jnp.concatenate(
            [
                lax.ppermute(tail, axis, [(i, (i + 1) % count) for i in range(ends)]),
                cells,
                lax.ppermute(head, axis, [((i + 1) % count, i) for i in range(ends)]),
            ],
            axis=dim,
        )
    return cells


def partner(value, axis, stride):
    mask = 2**stride
    pairs = [(source, source ^ mask) for source in range(lax.axis_size(axis))]
    return lax.ppermute(value, axis, pairs)


def in_blocks(array, dim, peers):
    dims = array.shape
    pieces = array.reshape(*dims[:dim], peers, dims[dim] // peers, *dims[dim + 1 :])
    return jnp.moveaxis(pieces, dim, 0)


def sum_at_owner(array, axis, dim):
    peers = lax.axis_size(axis)
    pieces = lax.all_to_all(in_blocks(array, dim, peers), axis, 0, 0, tiled=True)
    return jnp.sum(pieces, axis=0)


def split_product(form, wide, exact):
    leading = wide.astype(jnp.bfloat16)
    trailing = (wide - leading.astype(jnp.float32)).astype(jnp.bfloat16)
    first = jnp.einsum(form, leading, exact, preferred_element_type=jnp.float32)
    return first + jnp.einsum(form, trailing, exact, preferred_element_type=jnp.float32)


def near_tiles(targets, sources, coord_dim):
    target_norm = jnp.sum(jnp.square(targets.astype(jnp.float32)), axis=0)
    source_norm = jnp.sum(jnp.square(sources.astype(jnp.float32)), axis=0)
    cross = jnp.einsum("dpa,dpb->pab", targets, sources, preferred_element_type=jnp.float32)
    distance = target_norm[:, :, None] + source_norm[:, None, :] - 2.0 * cross
    return jnp.exp(distance * (-3.0 / coord_dim))


def inner_field(goals, gathered, coord_dim):
    places = gathered[:, :, :coord_dim]
    source_loads = gathered[:, :, coord_dim:]
    goal_norm = jnp.sum(jnp.square(goals.astype(jnp.float32)), axis=1)
    place_norm = jnp.sum(jnp.square(places.astype(jnp.float32)), axis=2)
    cross = jnp.einsum("ndt,nfds->nfts", goals, places, preferred_element_type=jnp.float32)
    distance = goal_norm[:, None, :, None] + place_norm[:, :, None, :] - 2.0 * cross
    kernel = jnp.exp(distance * (-3.0 / coord_dim)).astype(jnp.bfloat16)
    return jnp.einsum("nfrs,nfts->nrt", source_loads, kernel, preferred_element_type=jnp.float32)


def upper_field(goals, nodes_all, entries, coord_dim):
    gathered = jnp.take(nodes_all, entries, axis=1)
    places = gathered[:coord_dim]
    source_loads = gathered[coord_dim:]
    goal_norm = jnp.sum(jnp.square(goals.astype(jnp.float32)), axis=0)
    place_norm = jnp.sum(jnp.square(places.astype(jnp.float32)), axis=0)
    cross = jnp.einsum("dt,dfs->fts", goals, places, preferred_element_type=jnp.float32)
    distance = goal_norm[None, :, None] + place_norm[:, None, :] - 2.0 * cross
    kernel = jnp.exp(distance * (-3.0 / coord_dim)).astype(jnp.bfloat16)
    return jnp.einsum("rfs,fts->rt", source_loads, kernel, preferred_element_type=jnp.float32)


def on_device(
    points,
    charges,
    leaf_ids,
    inner_ids,
    upper_ids_first,
    upper_ids_second,
    upper_ids_third,
    leaf_maps,
    inner_maps,
    upper_maps_first,
    upper_maps_second,
    upper_maps_third,
    near_lists,
    far_inner,
    far_upper_first,
    far_upper_second,
    far_upper_third,
):
    coord_dim = points.shape[0]
    rhs_count = charges.shape[0]
    stacked = coord_dim + rhs_count
    leaf_count, skel_size, leaf_size = leaf_maps.shape
    local_points = leaf_count * leaf_size
    inner_levels = leaf_count.bit_length() - 1
    position = lax.axis_index("leaf")
    joined_input = jnp.concatenate([points, charges], axis=0)
    extended = extended_2(joined_input, (("leaf", 1),), local_points)
    window = extended.reshape(stacked, 3 * leaf_count, leaf_size)
    own_points = points.reshape(coord_dim, leaf_count, leaf_size)
    per_leaf = near_lists.shape[1]
    entries = near_lists.reshape(-1)
    owners = jnp.arange(entries.shape[0], dtype=jnp.int32) // per_leaf
    is_live = entries >= 0
    ranking = jnp.argsort(jnp.where(is_live, 0, 1).astype(jnp.int32), stable=True)
    entries = entries[ranking]
    owners = owners[ranking]
    is_live = is_live[ranking]
    live_count = jnp.sum(is_live.astype(jnp.int32))
    offsets = jnp.where(is_live, entries - (position - 1) * leaf_count, leaf_count)
    rounds = (live_count + pair_block - 1) // pair_block
    leaf_range = jnp.arange(leaf_count, dtype=jnp.int32)

    def near_round(round_index, running):
        first_slot = round_index * pair_block
        block_offsets = lax.dynamic_slice_in_dim(offsets, first_slot, pair_block)
        block_owners = lax.dynamic_slice_in_dim(owners, first_slot, pair_block)
        block_live = lax.dynamic_slice_in_dim(is_live, first_slot, pair_block).astype(jnp.float32)
        sources = jnp.take(window, block_offsets, axis=1)
        targets = jnp.take(own_points, block_owners, axis=1)
        kernel = (
            near_tiles(targets, sources[:coord_dim], coord_dim) * block_live[:, None, None]
        ).astype(jnp.bfloat16)
        pair_terms = jnp.einsum(
            "rpb,pab->pra", sources[coord_dim:], kernel, preferred_element_type=jnp.float32
        )
        select = (block_owners[:, None] == leaf_range[None, :]).astype(jnp.bfloat16)
        return running + split_product("pra,pt->rta", pair_terms, select)

    near_part = lax.fori_loop(
        0, rounds, near_round, jnp.zeros((rhs_count, leaf_count, leaf_size), jnp.float32)
    )
    leaf_coords = jnp.take_along_axis(own_points, leaf_ids[None], axis=2).transpose(1, 0, 2)
    leaf_weights = jnp.einsum(
        "rnp,nsp->nrs",
        charges.reshape(rhs_count, leaf_count, leaf_size),
        leaf_maps,
        preferred_element_type=jnp.float32,
    ).astype(jnp.bfloat16)
    stacks = [jnp.concatenate([leaf_coords, leaf_weights], axis=1)]
    for degree in range(1, inner_levels + 1):
        node_count = leaf_count >> degree
        offset_row = leaf_count - 2 * node_count
        paired = stacks[-1].reshape(node_count, 2, stacked, skel_size).transpose(0, 2, 1, 3)
        paired = paired.reshape(node_count, stacked, 2 * skel_size)
        chosen = inner_ids[offset_row : offset_row + node_count]
        coords = jnp.take_along_axis(paired[:, :coord_dim], chosen[:, None, :], axis=2)
        weights = jnp.einsum(
            "nrk,nsk->nrs",
            paired[:, coord_dim:],
            inner_maps[offset_row : offset_row + node_count],
            preferred_element_type=jnp.float32,
        ).astype(jnp.bfloat16)
        stacks.append(jnp.concatenate([coords, weights], axis=1))
    far_terms = []
    for degree in range(inner_levels):
        node_count = leaf_count >> degree
        offset_row = 2 * leaf_count - 2 * node_count
        rimmed_nodes = extended_2(stacks[degree], (("leaf", 0),), node_count)
        local_entries = (
            far_inner[offset_row : offset_row + node_count] - (position - 1) * node_count
        )
        gathered = jnp.take(rimmed_nodes, local_entries, axis=0)
        far_terms.append(inner_field(stacks[degree][:, :coord_dim], gathered, coord_dim))
    root = stacks[inner_levels][0]
    root_entries = far_inner[2 * leaf_count - 2]
    uppers = (
        (upper_ids_first, upper_maps_first, far_upper_first),
        (upper_ids_second, upper_maps_second, far_upper_second),
        (upper_ids_third, upper_maps_third, far_upper_third),
    )
    shares = [root]
    gathered_tiers = []
    for degree in range(4):
        if degree > 0:
            group_size = 1 << degree
            share_rows = skel_size // group_size
            ancestor = position >> degree
            member = position % group_size
            paired = lax.dynamic_slice_in_dim(gathered_tiers[-1], 2 * ancestor, 2, 1)
            paired = paired.reshape(stacked, 2 * skel_size)
            full_ids = lax.dynamic_index_in_dim(uppers[degree - 1][0], ancestor, 0, keepdims=False)
            chosen = lax.dynamic_slice_in_dim(full_ids, member * share_rows, share_rows)
            coords = jnp.take(paired[:coord_dim], chosen, axis=1)
            weights = jnp.einsum(
                "rk,sk->rs",
                paired[coord_dim:],
                uppers[degree - 1][1],
                preferred_element_type=jnp.float32,
            ).astype(jnp.bfloat16)
            shares.append(jnp.concatenate([coords, weights], axis=0))
        everything = lax.all_gather(shares[-1], "leaf", axis=1, tiled=True)
        gathered_tiers.append(everything.reshape(stacked, -1, skel_size))
    root_term = upper_field(root[:coord_dim], gathered_tiers[0], root_entries, coord_dim)
    incoming = None
    for degree in range(3, 0, -1):
        group_size = 1 << degree
        share_rows = skel_size // group_size
        member = position % group_size
        ancestor = position >> degree
        entries_here = lax.dynamic_index_in_dim(uppers[degree - 1][2], ancestor, 0, keepdims=False)
        level_term = upper_field(
            shares[degree][:coord_dim], gathered_tiers[degree], entries_here, coord_dim
        )
        if incoming is not None:
            level_term = level_term + lax.dynamic_slice_in_dim(
                incoming, member * share_rows, share_rows, 1
            )
        spread = split_product("rs,sk->rk", level_term, uppers[degree - 1][1])
        for bit_index in range(degree):
            spread = spread + partner(spread.astype(jnp.bfloat16), "leaf", bit_index).astype(
                spread.dtype
            )
        branch = position >> degree - 1 & 1
        incoming = lax.dynamic_slice_in_dim(spread, branch * skel_size, skel_size, 1)
    root_total = root_term + incoming
    totals = root_total[None]
    for degree in range(inner_levels, 0, -1):
        node_count = leaf_count >> degree
        offset_row = leaf_count - 2 * node_count
        spread = split_product(
            "nrs,nsk->nrk", totals, inner_maps[offset_row : offset_row + node_count]
        )
        children = spread.reshape(node_count, rhs_count, 2, skel_size).transpose(0, 2, 1, 3)
        children = children.reshape(2 * node_count, rhs_count, skel_size)
        totals = far_terms[degree - 1] + children
    far_part = split_product("nrs,nsp->rnp", totals, leaf_maps)
    result = (near_part + far_part).reshape(rhs_count, local_points)
    return sum_at_owner(result, "list", 1)


def solution(mesh):
    placed = (
        P(None, "leaf"),
        P(None, "leaf"),
        P("leaf", None),
        P("leaf", None),
        P(),
        P(),
        P(),
        P("leaf", None, None),
        P("leaf", None, None),
        P("leaf", None),
        P("leaf", None),
        P("leaf", None),
        P("leaf", "list"),
        P("leaf", "list"),
        P(None, "list"),
        P(None, "list"),
        P(None, "list"),
    )
    return jax.shard_map(
        on_device, mesh=mesh, in_specs=placed, out_specs=P(None, ("leaf", "list")), check_vma=False
    )
```

profile of v0, /device:TPU:9, one launch (start us, length us, event | category | flops | bytes accessed | tf_op | source)
XLA Modules:
  0.0 439.7 jit_solution(10743653224097981592)
XLA Ops:
  10.0 2.6 collective-permute-start.1
  12.6 3.1 collective-permute-start
  18.6 20.5 %gather_fusion.17 = bf16[2048,32]{1,0:T(8,128)(2,1)} fusion(bf16[32,16,256]{0,2,1:T(8,128)(2,1)S(1)} %bitcast.432, s32[2048]{0:T(1024)S(1)} %fusion.219), kind=kCustom, calls=%fused_computation.17 | custom fusion | bytes 278528 | tf_op jit(solution)/shard_map/jit(take_along_axis)/gather | solution.py:144
  48.9 17.1 %gather_fusion.18 = bf16[1024,32]{1,0:T(8,128)(2,1)} fusion(bf16[8,32,256]{1,2,0:T(8,128)(2,1)} %copy.189, s32[1024]{0:T(1024)S(1)} %fusion.227), kind=kCustom, calls=%fused_computation.18 | custom fusion | bytes 139264 | tf_op jit(solution)/shard_map/jit(take_along_axis)/gather | solution.py:158
  71.1 5.5 %gather_fusion.19 = bf16[512,32]{1,0:T(8,128)(2,1)} fusion(bf16[4,32,256]{1,2,0:T(8,128)(2,1)S(1)} %copy.196, s32[512]{0:T(512)S(1)} %fusion.241), kind=kCustom, calls=%fused_computation.19 | custom fusion | bytes 69632 | tf_op jit(solution)/shard_map/jit(take_along_axis)/gather | solution.py:158
  83.0 6.6 %collective-permute-start.9 = (bf16[2,64,128]{2,1,0:T(8,128)(2,1)S(1)}, bf16[2,64,128]{2,1,0:T(8,128)(2,1)S(1)}, u32[]{:S(2)}, u32[]{:S(2)}) collective-permute-start(bf16[2,64,128]{2,1,0:T(8,128)(2,1)S(1)} %get-tuple-element.176), channel_id=1, source_target_pairs={{4,0},{8,4},{12,8},{16,12},{20,16},{24,20},{28,24},{32,28},{36,32}... | collective-permute-start | bytes 98312 | tf_op jit(solution)/shard_map/ppermute | solution.py:19
  106.8 2.5 sort.17
  122.0 3.4 collective-permute-start.7
  125.4 2.3 collective-permute-start.6
  129.9 3.3 collective-permute-start.5
  133.1 2.3 collective-permute-start.4
  137.1 2.1 collective-permute-start.2
  143.7 2.2 gather_fusion.5
  151.9 26.8 %all-gather.6.cloned.1.call-done = bf16[1,64,16384]{2,1,0:T(8,128)(2,1)} async-done(((bf16[1,64,128]{2,1,0:T(8,128)(2,1)}), bf16[1,64,16384]{2,1,0:T(8,128)(2,1)}) %all-gather.6.cloned.1.call-update) | async-done | bytes 2097168 | tf_op jit(solution)/shard_map/all_gather | solution.py:203
  178.7 2.2 copy.259
  184.8 43.3 %while.11 = (s32[]{:T(128)}, f32[32,16,256]{2,1,0:T(8,128)S(1)}, s32[]{:T(128)}, s32[128]{0:T(128)}, s32[128]{0:T(128)S(1)}, /*index=5*/bf16[64,48,256]{2,0,1:T(...) while((s32[]{:T(128)}, f32[32,16,256]{2,1,0:T(8,128)S(1)}, ...), condition=%wide.region_5.6_spmd.clone, body=%wide.region_2.5_spmd.clone.sunk | while | flops 150989568 | bytes 7152779 | solution.py:141
  228.1 4.3 copy.211
  232.5 2.3 gather_fusion.10
  234.8 28.6 %all-gather.4.cloned.1.call-done = bf16[64,8192]{0,1:T(8,128)(2,1)} async-done(((bf16[64,64]{0,1:T(8,128)(2,1)}), bf16[64,8192]{0,1:T(8,128)(2,1)}) %all-gather.4.cloned.1.call-update) | async-done | bytes 1048592 | tf_op jit(solution)/shard_map/all_gather | solution.py:203
  266.0 49.5 %all_gather.14 = bf16[64,4096]{0,1:T(8,128)(2,1)S(1)} all-gather(bf16[64,32]{0,1:T(8,128)(2,1)S(1)} %pad_maximum_fusion.15), channel_id=1, replica_groups=mesh['leaf'=128,'list'=4] {'leaf'}, dimensions={1}, use_global_device_ids=true | all-gather | bytes 528384 | tf_op jit(solution)/shard_map/all_gather | solution.py:203
  317.3 48.5 %all_gather.15 = bf16[64,2048]{0,1:T(8,128)(2,1)S(1)} all-gather(bf16[64,16]{0,1:T(8,128)(2,1)S(1)} %pad_maximum_fusion.16), channel_id=1, replica_groups=mesh['leaf'=128,'list'=4] {'leaf'}, dimensions={1}, use_global_device_ids=true | all-gather | bytes 264192 | tf_op jit(solution)/shard_map/all_gather | solution.py:203
  370.3 2.1 collective-permute-start.10
  374.9 2.9 collective-permute-start.11
  379.4 4.3 collective-permute-start.12
  383.8 2.7 copy.217
  386.5 2.0 gather_fusion.12
  389.2 3.7 collective-permute-start.13
  393.7 2.5 collective-permute-start.14
  399.5 3.4 collective-permute-start.15
  409.1 3.1 fusion.68
  413.1 5.0 %fusion.58 = f32[16,32,128]{2,1,0:T(8,128)S(1)} fusion(f32[16,32,128]{2,1,0:T(8,128)S(1)} %bitcast.458, f32[16,8,128]{2,1,0:T(8,128)S(1)} %copy-done.31, f32[16,128]{1,0:T(8,128)S(1)} %copy-done.47, bf16[16,8,64,128]{3,2,1,0:T(8,128)(2,1)} %copy-done.2, bf16[16,128,32]{1,2,0:T(8,128)(2,1)S(1)} %copy-done.15, pred[16,128]{1,0:T(8,128)(4,1)S(1)} %copy-done.46), kind=kOutput, calls=%fused_computation.96 | convolution fusion | flops 279052288 | bytes 2828288 | tf_op jit(solution)/shard_map/nfrs,nfts->nrt/dot_general | solution.py:67
  419.7 12.4 %all_to_all.5 = f32[4,32,1024]{2,1,0:T(8,128)S(1)} all-to-all(f32[4,32,1024]{2,1,0:T(8,128)S(1)} %copy.223), channel_id=1, replica_groups=mesh['leaf'=128,'list'=4] {'list'}, dimensions={0} | all-to-all | bytes 1048576 | tf_op jit(solution)/shard_map/all_to_all | solution.py:40
  (428 shorter events, 143.9 us)
Async XLA Ops:
  6.5 34.5 %copy-start = (bf16[16,128,256]{2,1,0:T(8,128)(2,1)S(1)}, bf16[16,128,256]{2,1,0:T(8,128)(2,1)}, u32[]{:S(2)}) copy-start(bf16[16,128,256]{2,1,0:T(8,128)(2,1)} %param.26) | copy-start | bytes 3145732
  6.5 172.1 %all-gather.6.cloned.1.call-start = ((), (), s32[]{:S(2)}) async-start(), calls=%async_computation.2 | async-start | bytes 2113536 | tf_op jit(solution)/shard_map/all_gather | solution.py:203
  10.0 139.1 %collective-permute-start.1 = (bf16[64,4096]{1,0:T(8,128)(2,1)}, bf16[64,4096]{1,0:T(8,128)(2,1)}, u32[]{:S(2)}, u32[]{:S(2)}) collective-permute-start(bf16[64,4096]{1,0:T(8,128)(2,1)} %constant_dynamic-update-slice_fusion), channel_id=1, source_target_pairs={{4,0},{8,4},{12,8},{16,12},{20,16},{24,20},{28,24},{32,28},{36,32}... | collective-permute-start | bytes 1572872 | tf_op jit(solution)/shard_map/ppermute | solution.py:19
  12.6 136.5 %collective-permute-start = (bf16[64,4096]{1,0:T(8,128)(2,1)}, bf16[64,4096]{1,0:T(8,128)(2,1)}, u32[]{:S(2)}, u32[]{:S(2)}) collective-permute-start(bf16[64,4096]{1,0:T(8,128)(2,1)} %constant_dynamic-update-slice_fusion), channel_id=1, source_target_pairs={{0,4},{4,8},{8,12},{12,16},{16,20},{20,24},{24,28},{28,32},{32,36}... | collective-permute-start | bytes 1572872 | tf_op jit(solution)/shard_map/ppermute | solution.py:17
  16.4 25.1 %copy-start.45 = (pred[16,128]{1,0:T(8,128)(4,1)}, pred[16,128]{1,0:T(8,128)(4,1)S(1)}, u32[]{:S(2)}) copy-start(pred[16,128]{1,0:T(8,128)(4,1)S(1)} %compare_and_fusion.2) | copy-start | bytes 6148
  18.6 27.2 %copy-start.42 = (s32[15,128]{1,0:T(8,128)S(1)}, s32[15,128]{1,0:T(8,128)}, u32[]{:S(2)}) copy-start(s32[15,128]{1,0:T(8,128)} %param.22) | copy-start | bytes 23044
  41.5 25.6 %copy-start.8 = (bf16[16,32,128]{2,1,0:T(8,128)(2,1)}, bf16[16,32,128]{2,1,0:T(8,128)(2,1)S(1)}, u32[]{:S(2)}) copy-start(bf16[16,32,128]{2,1,0:T(8,128)(2,1)S(1)} %convolution_convert_fusion) | copy-start | bytes 393220
  43.9 97.3 %collective-permute-start.3 = (bf16[16,64,128]{2,1,0:T(8,128)(2,1)}, bf16[16,64,128]{2,1,0:T(8,128)(2,1)}, u32[]{:S(2)}, u32[]{:S(2)}) collective-permute-start(bf16[16,64,128]{2,1,0:T(8,128)(2,1)} %pad_maximum_fusion.3), channel_id=1, source_target_pairs={{4,0},{8,4},{12,8},{16,12},{20,16},{24,20},{28,24},{32,28},{36,32}... | collective-permute-start | bytes 786440 | tf_op jit(solution)/shard_map/ppermute | solution.py:19
  45.8 36.7 %copy-start.58 = (pred[2,128]{1,0:T(4,128)(4,1)}, pred[2,128]{1,0:T(4,128)(4,1)S(1)}, u32[]{:S(2)}) copy-start(pred[2,128]{1,0:T(4,128)(4,1)S(1)} %compare_and_fusion.16) | copy-start | bytes 772
  45.8 31.8 %copy-start.51 = (pred[4,128]{1,0:T(4,128)(4,1)}, pred[4,128]{1,0:T(4,128)(4,1)S(1)}, u32[]{:S(2)}) copy-start(pred[4,128]{1,0:T(4,128)(4,1)S(1)} %compare_and_fusion.17) | copy-start | bytes 1540
  67.1 29.8 %copy-start.28 = (s32[31,8]{0,1:T(8,128)S(1)}, s32[31,8]{0,1:T(8,128)}, u32[]{:S(2)}) copy-start(s32[31,8]{0,1:T(8,128)} %param.32) | copy-start | bytes 2980
  82.5 46.6 %copy-start.32 = (bf16[2,128,32]{1,2,0:T(8,128)(2,1)}, bf16[2,128,32]{1,2,0:T(8,128)(2,1)S(1)}, u32[]{:S(2)}) copy-start(bf16[2,128,32]{1,2,0:T(8,128)(2,1)S(1)} %copy.205) | copy-start | bytes 49156
  83.0 38.9 %collective-permute-start.9 = (bf16[2,64,128]{2,1,0:T(8,128)(2,1)S(1)}, bf16[2,64,128]{2,1,0:T(8,128)(2,1)S(1)}, u32[]{:S(2)}, u32[]{:S(2)}) collective-permute-start(bf16[2,64,128]{2,1,0:T(8,128)(2,1)S(1)} %get-tuple-element.176), channel_id=1, source_target_pairs={{4,0},{8,4},{12,8},{16,12},{20,16},{24,20},{28,24},{32,28},{36,32}... | collective-permute-start | bytes 98312 | tf_op jit(solution)/shard_map/ppermute | solution.py:19
  89.6 35.8 %collective-permute-start.8 = (bf16[2,64,128]{2,1,0:T(8,128)(2,1)S(1)}, bf16[2,64,128]{2,1,0:T(8,128)(2,1)}, u32[]{:S(2)}, u32[]{:S(2)}) collective-permute-start(bf16[2,64,128]{2,1,0:T(8,128)(2,1)S(1)} %get-tuple-element.176), channel_id=1, source_target_pairs={{0,4},{4,8},{8,12},{12,16},{16,20},{20,24},{24,28},{28,32},{32,36}... | collective-permute-start | bytes 98312 | tf_op jit(solution)/shard_map/ppermute | solution.py:17
  94.0 26.2 %copy-start.30 = (bf16[128,32]{0,1:T(8,128)(2,1)}, bf16[128,32]{0,1:T(8,128)(2,1)S(1)}, u32[]{:S(2)}) copy-start(bf16[128,32]{0,1:T(8,128)(2,1)S(1)} %copy.210) | copy-start | bytes 24580
  94.7 168.7 %all-gather.4.cloned.1.call-start = ((), (), s32[]{:S(2)}) async-start(), calls=%async_computation.1 | async-start | bytes 2113536 | tf_op jit(solution)/shard_map/all_gather | solution.py:203
  122.0 7.9 %collective-permute-start.7 = (bf16[4,64,128]{2,1,0:T(8,128)(2,1)S(1)}, bf16[4,64,128]{2,1,0:T(8,128)(2,1)S(1)}, u32[]{:S(2)}, u32[]{:S(2)}) collective-permute-start(bf16[4,64,128]{2,1,0:T(8,128)(2,1)S(1)} %pad_maximum_fusion.9), channel_id=1, source_target_pairs={{4,0},{8,4},{12,8},{16,12},{20,16},{24,20},{28,24},{32,28},{36,32}... | collective-permute-start | bytes 196616 | tf_op jit(solution)/shard_map/ppermute | solution.py:19
  125.4 7.8 %collective-permute-start.6 = (bf16[4,64,128]{2,1,0:T(8,128)(2,1)S(1)}, bf16[4,64,128]{2,1,0:T(8,128)(2,1)S(1)}, u32[]{:S(2)}, u32[]{:S(2)}) collective-permute-start(bf16[4,64,128]{2,1,0:T(8,128)(2,1)S(1)} %pad_maximum_fusion.9), channel_id=1, source_target_pairs={{0,4},{4,8},{8,12},{12,16},{16,20},{20,24},{24,28},{28,32},{32,36}... | collective-permute-start | bytes 196616 | tf_op jit(solution)/shard_map/ppermute | solution.py:17
  129.9 7.2 %collective-permute-start.5 = (bf16[8,64,128]{2,1,0:T(8,128)(2,1)S(1)}, bf16[8,64,128]{2,1,0:T(8,128)(2,1)S(1)}, u32[]{:S(2)}, u32[]{:S(2)}) collective-permute-start(bf16[8,64,128]{2,1,0:T(8,128)(2,1)S(1)} %copy-done.17), channel_id=1, source_target_pairs={{4,0},{8,4},{12,8},{16,12},{20,16},{24,20},{28,24},{32,28},{36,32}... | collective-permute-start | bytes 393224 | tf_op jit(solution)/shard_map/ppermute | solution.py:19
  133.1 6.0 %collective-permute-start.4 = (bf16[8,64,128]{2,1,0:T(8,128)(2,1)S(1)}, bf16[8,64,128]{2,1,0:T(8,128)(2,1)S(1)}, u32[]{:S(2)}, u32[]{:S(2)}) collective-permute-start(bf16[8,64,128]{2,1,0:T(8,128)(2,1)S(1)} %copy-done.17), channel_id=1, source_target_pairs={{0,4},{4,8},{8,12},{12,16},{16,20},{20,24},{24,28},{28,32},{32,36}... | collective-permute-start | bytes 393224 | tf_op jit(solution)/shard_map/ppermute | solution.py:17
  137.1 5.5 %collective-permute-start.2 = (bf16[16,64,128]{2,1,0:T(8,128)(2,1)}, bf16[16,64,128]{2,1,0:T(8,128)(2,1)}, u32[]{:S(2)}, u32[]{:S(2)}) collective-permute-start(bf16[16,64,128]{2,1,0:T(8,128)(2,1)} %pad_maximum_fusion.3), channel_id=1, source_target_pairs={{0,4},{4,8},{8,12},{12,16},{16,20},{20,24},{24,28},{28,32},{32,36}... | collective-permute-start | bytes 786440 | tf_op jit(solution)/shard_map/ppermute | solution.py:17
  228.1 37.0 %copy-start.24 = (bf16[32,256]{1,0:T(8,128)(2,1)S(1)}, bf16[32,256]{1,0:T(8,128)(2,1)}, u32[]{:S(2)}) copy-start(bf16[32,256]{1,0:T(8,128)(2,1)} %param.29) | copy-start | bytes 49156
  228.1 37.1 %copy-start.55 = (pred[32]{0:T(512)(128)(4,1)S(1)}, pred[32]{0:T(512)(128)(4,1)}, u32[]{:S(2)}) copy-start(pred[32]{0:T(512)(128)(4,1)} %compare_and_fusion.10) | copy-start | bytes 100
  232.5 83.9 %copy-start.29 = (bf16[16,256]{1,0:T(8,128)(2,1)S(1)}, bf16[16,256]{1,0:T(8,128)(2,1)}, u32[]{:S(2)}) copy-start(bf16[16,256]{1,0:T(8,128)(2,1)} %param.30) | copy-start | bytes 24580
  232.5 84.0 %copy-start.57 = (pred[16]{0:T(512)(128)(4,1)S(1)}, pred[16]{0:T(512)(128)(4,1)}, u32[]{:S(2)}) copy-start(pred[16]{0:T(512)(128)(4,1)} %compare_and_fusion.8) | copy-start | bytes 52
  265.1 50.6 %copy-start.38 = (bf16[32,32]{1,0:T(8,128)(2,1)}, bf16[32,32]{1,0:T(8,128)(2,1)S(1)}, u32[]{:S(2)}) copy-start(bf16[32,32]{1,0:T(8,128)(2,1)S(1)} %gather_fusion.13) | copy-start | bytes 6148
  370.3 4.6 %collective-permute-start.10 = (bf16[32,256]{1,0:T(8,128)(2,1)S(1)}, bf16[32,256]{1,0:T(8,128)(2,1)S(1)}, u32[]{:S(2)}, u32[]{:S(2)}) collective-permute-start(bf16[32,256]{1,0:T(8,128)(2,1)S(1)} %get-tuple-element.182), channel_id=1, source_target_pairs={{0,4},{4,0},{8,12},{12,8},{16,20},{20,16},{24,28},{28,24},{32,36},... | collective-permute-start | bytes 49160 | tf_op jit(solution)/shard_map/ppermute | solution.py:29
  374.9 4.5 %collective-permute-start.11 = (bf16[32,256]{1,0:T(8,128)(2,1)S(1)}, bf16[32,256]{1,0:T(8,128)(2,1)S(1)}, u32[]{:S(2)}, u32[]{:S(2)}) collective-permute-start(bf16[32,256]{1,0:T(8,128)(2,1)S(1)} %fusion.182), channel_id=1, source_target_pairs={{0,8},{4,12},{8,0},{12,4},{16,24},{20,28},{24,16},{28,20},{32,40},... | collective-permute-start | bytes 49160 | tf_op jit(solution)/shard_map/ppermute | solution.py:29
  379.4 9.2 %collective-permute-start.12 = (bf16[32,256]{1,0:T(8,128)(2,1)S(1)}, bf16[32,256]{1,0:T(8,128)(2,1)S(1)}, u32[]{:S(2)}, u32[]{:S(2)}) collective-permute-start(bf16[32,256]{1,0:T(8,128)(2,1)S(1)} %get-tuple-element.159), channel_id=1, source_target_pairs={{0,16},{4,20},{8,24},{12,28},{16,0},{20,4},{24,8},{28,12},{32,48},... | collective-permute-start | bytes 49160 | tf_op jit(solution)/shard_map/ppermute | solution.py:29
  389.2 4.5 %collective-permute-start.13 = (bf16[32,256]{1,0:T(8,128)(2,1)S(1)}, bf16[32,256]{1,0:T(8,128)(2,1)S(1)}, u32[]{:S(2)}, u32[]{:S(2)}) collective-permute-start(bf16[32,256]{1,0:T(8,128)(2,1)S(1)} %get-tuple-element.184), channel_id=1, source_target_pairs={{0,4},{4,0},{8,12},{12,8},{16,20},{20,16},{24,28},{28,24},{32,36},... | collective-permute-start | bytes 49160 | tf_op jit(solution)/shard_map/ppermute | solution.py:29
  393.7 4.5 %collective-permute-start.14 = (bf16[32,256]{1,0:T(8,128)(2,1)S(1)}, bf16[32,256]{1,0:T(8,128)(2,1)S(1)}, u32[]{:S(2)}, u32[]{:S(2)}) collective-permute-start(bf16[32,256]{1,0:T(8,128)(2,1)S(1)} %get-tuple-element.155), channel_id=1, source_target_pairs={{0,8},{4,12},{8,0},{12,4},{16,24},{20,28},{24,16},{28,20},{32,40},... | collective-permute-start | bytes 49160 | tf_op jit(solution)/shard_map/ppermute | solution.py:29
  399.5 4.2 collective-permute-start.15
  (49 other events, 416.0 us)
Sparse Core Ops, SparseCore 0:
  94.8 83.8 all-gather.5
  184.8 78.4 all-gather.3
where the time goes:
time: 444 us; the launch traced here: 440 us
  local copies, waits for them, and re-layouts  115 us (26%)
  blocking collectives  110 us (25%)
  waiting for transfers between devices  61.6 us (14%)
  other arithmetic  49.7 us (11%)
  starting transfers between devices  48.3 us (11%)
  matrix products  38.2 us (9%)
  between operations  15.5 us (3%)
    all_gather x2, blocking collectives, on_device(): everything = lax.all_gather(shares[-1], 'leaf', axis=1, tiled=True)  98.1 us
    all_gather x2, waiting for transfers between devices, on_device(): everything = lax.all_gather(shares[-1], 'leaf', axis=1, tiled=True)  55.3 us
    gather x8, local copies, waits for them, and re-layouts, on_device(): jnp.take_along_axis(paired[:, :coord_dim], chosen[:, None, :], axis=2)  27.2 us
    gather x2, local copies, waits for them, and re-layouts, on_device(): jnp.take_along_axis(own_points, leaf_ids[None], axis=2).transpose(1, 0, 2)  22.5 us
    ppermute x6, starting transfers between devices, partner(): return lax.ppermute(value, axis, pairs)  18.9 us
    ppermute x5, starting transfers between devices, extended_2(): lax.ppermute(head, axis, [((i + 1) % count, i) for i in range(ends)])  17.7 us
    gather x7, local copies, waits for them, and re-layouts, near_round(): sources = jnp.take(window, block_offsets, axis=1)  13.9 us
    dot_general x7, matrix products, near_round(): jnp.einsum('rpb,pab->pra', sources[coord_dim:], kernel, preferred_element...  12.7 us
  transfers between devices with their start and end apart: 18, of which 7 were waited for; matrix products, arithmetic and copies ran while one was open for 38% of the time, Pallas kernels for 0%

commit v1 on v0

v1 whole, which is shorter than its diff:
```python
import functools
import math

import jax
import jax.numpy as jnp
from jax import lax
from jax.experimental import pallas as pl
from jax.experimental.pallas import tpu as pltpu
from jax.sharding import PartitionSpec as P

MESH = pl.DeviceIdType.MESH
BF16 = jnp.bfloat16
F32 = jnp.float32
VMEM = pl.BlockSpec(memory_space=pltpu.VMEM)
SMEM = pl.BlockSpec(memory_space=pltpu.SMEM)
UNROLL = 4
NODES = 31
OFFSETS = (0, 16, 24, 28, 30)
RATE = -3.0 / 32.0 * math.log2(math.e)
NT = (((1,), (1,)), ((), ()))


def dot(a, b):
    return jnp.dot(a, b, preferred_element_type=F32)


def dot_nt(a, b):
    return lax.dot_general(a, b, NT, preferred_element_type=F32)


def climb(pair, ids, mat):
    rows = lax.broadcasted_iota(jnp.int32, (256, 128), 0)
    hot = jnp.where(rows == ids, 1.0, 0.0).astype(BF16)
    coords = dot(pair[:32], hot).astype(BF16)
    weights = dot_nt(pair[32:], mat).astype(BF16)
    return coords, weights


def gather_kernel(
    points, charges, leaf_ids, inner_ids, ids5, ids6, ids7, leaf_maps, inner_maps,
    maps5, maps6, maps7, near, far5, far6, far7,
    side_points, side_charges, nodes, side_nodes, all5, all6, all7, near_all, own_upper, chosen,
    roots, group5, group6, group7, half5, half6, half7, sent, buf5, buf6, buf7,
    map_send, map_recv, list_send, list_recv, root_send, root_recv, side_send, side_recv,
    ring_send, ring_recv, swap_send, swap_recv,
):
    leaf = lax.axis_index("leaf")
    plane = lax.axis_index("list")
    core = leaf % 2
    y = (leaf // 2) % 8
    z = leaf // 16
    g = leaf % 8
    base8 = leaf - g
    sides = ((leaf + 127) % 128, (leaf + 1) % 128)
    group = [base8 + (g + k) % 8 for k in range(1, 8)]
    row = [z * 16 + ((y + k) % 8) * 2 + core for k in range(1, 8)]
    column = [((z + k) % 8) * 16 + y * 2 + core for k in range(1, 8)]
    sibling = leaf + 1 - 2 * core

    def to(who):
        return (who, plane)

    barrier = pltpu.get_barrier_semaphore()
    peers = [to(w) for w in (*sides, *group, *row, *column)]
    peers += [(leaf, (plane + k) % 4) for k in range(1, 4)]
    for who in peers:
        pl.semaphore_signal(barrier, inc=1, device_id=who, device_id_type=MESH)
    pl.semaphore_wait(barrier, len(peers))

    copies = []

    def send(src, dst, s_sem, r_sem, who):
        copy = pltpu.make_async_remote_copy(
            src_ref=src, dst_ref=dst, send_sem=s_sem, recv_sem=r_sem, device_id=who, device_id_type=MESH
        )
        copy.start()
        copies.append(copy)
        return copy

    map_copies = []
    for k in range(1, 8):
        for level, (src, dst) in enumerate(((maps5, all5), (maps6, all6), (maps7, all7))):
            map_copies.append(
                send(src, dst.at[g], map_send.at[level, k], map_recv.at[level, k], to(group[k - 1]))
            )
    list_copies = [
        send(near, near_all.at[plane], list_send.at[k], list_recv.at[k], (leaf, (plane + k) % 4))
        for k in range(1, 4)
    ]
    all5[g] = maps5[...]
    all6[g] = maps6[...]
    all7[g] = maps7[...]
    near_all[plane] = near[...]

    for i in range(16):
        cols = slice(i * 256, (i + 1) * 256)
        pair = jnp.concatenate([points[:, cols], charges[:, cols]], axis=0)
        coords, weights = climb(pair, leaf_ids[i : i + 1, :], leaf_maps[i])
        nodes[i, :32] = coords
        nodes[i, 32:] = weights
    for level in range(1, 5):
        for i in range(16 >> level):
            child = OFFSETS[level - 1] + 2 * i
            here = OFFSETS[level] + i
            pair = jnp.concatenate([nodes[child], nodes[child + 1]], axis=1)
            coords, weights = climb(pair, inner_ids[here - 16 : here - 15, :], inner_maps[here - 16])
            nodes[here, :32] = coords
            nodes[here, 32:] = weights
    roots[g] = nodes[30]

    root_copies = [
        send(roots.at[g], roots.at[g], root_send.at[k], root_recv.at[k], to(group[k - 1]))
        for k in range(1, 8)
    ]
    side_copies = []
    for way in range(2):
        dst = 1 - way
        for n, (src, out) in enumerate(
            ((nodes, side_nodes), (points, side_points), (charges, side_charges))
        ):
            side_copies.append(
                send(src, out.at[dst], side_send.at[way, n], side_recv.at[way, n], to(sides[way]))
            )

    for copy in map_copies + root_copies:
        copy.wait_recv()

    def keep(dst, j, coords, weights):
        dst[j, :32] = coords
        dst[j, 32:] = weights

    quad = leaf // 8
    for j in range(4):
        pair = jnp.concatenate([roots[2 * j], roots[2 * j + 1]], axis=1)
        mat = jnp.concatenate([all5[2 * j], all5[2 * j + 1]], axis=0)
        keep(group5, j, *climb(pair, ids5[pl.ds(quad * 4 + j, 1), :], mat))
    for j in range(2):
        pair = jnp.concatenate([group5[2 * j], group5[2 * j + 1]], axis=1)
        mat = jnp.concatenate([all6[4 * j + n] for n in range(4)], axis=0)
        keep(group6, j, *climb(pair, ids6[pl.ds(quad * 2 + j, 1), :], mat))
    pair = jnp.concatenate([group6[0], group6[1]], axis=1)
    mat = jnp.concatenate([all7[n] for n in range(8)], axis=0)
    keep(group7, 0, *climb(pair, ids7[pl.ds(quad, 1), :], mat))

    mine = (group5[g // 2], group6[g // 4], group7[0])
    halves = (half5, half6, half7)
    for level in range(3):
        own_upper[level] = mine[level][:32]

    def put_half(c):
        for level in range(3):
            halves[level][:16] = mine[level][16 * c : 16 * c + 16]
            halves[level][16:] = mine[level][32 + 16 * c : 48 + 16 * c]

    @pl.when(core == 0)
    def _():
        put_half(0)
        slots = (leaf // 2, leaf // 4, leaf // 8)
        bufs = (buf5, buf6, buf7)
        ks = (range(1, 8), (2, 4, 6), (4,))
        first = []
        for level in range(3):
            for k in ks[level]:
                first.append(
                    send(
                        halves[level], bufs[level].at[slots[level]],
                        ring_send.at[0, level, k], ring_recv.at[0, level, k], to(row[k - 1]),
                    )
                )
            bufs[level][slots[level]] = halves[level][...]
        second = []
        for level in range(3):
            for copy in first:
                pass
        at = 0
        for level in range(3):
            for _k in ks[level]:
                first[at].wait_recv()
                at += 1
            size = 8 >> level
            slab = bufs[level].at[pl.ds(z * size, size)]
            for k in range(1, 8):
                second.append(
                    send(slab, slab, ring_send.at[1, level, k], ring_recv.at[1, level, k], to(column[k - 1]))
                )
        for copy in second:
            copy.wait_recv()
        for copy in first + second:
            copy.wait_send()

    @pl.when(core == 1)
    def _():
        put_half(1)
        slots = (y * 8 + z, (y // 2) * 8 + z, (y // 4) * 8 + z)
        bufs = (buf5, buf6, buf7)
        ks = (range(1, 8), (2, 4, 6), (4,))
        first = []
        for level in range(3):
            for k in range(1, 8):
                first.append(
                    send(
                        halves[level], bufs[level].at[slots[level]],
                        ring_send.at[0, level, k], ring_recv.at[0, level, k], to(column[k - 1]),
                    )
                )
            bufs[level][slots[level]] = halves[level][...]
        second = []
        for level in range(3):
            for k in range(7):
                first[level * 7 + k].wait_recv()
            slab = bufs[level].at[pl.ds((y // (1 << level)) * 8, 8)]
            for k in ks[level]:
                second.append(
                    send(slab, slab, ring_send.at[1, level, k], ring_recv.at[1, level, k], to(row[k - 1]))
                )
        for copy in second:
            copy.wait_recv()
        for copy in first + second:
            copy.wait_send()

    for f in range(8):
        n5 = far5[leaf // 2, f]
        n6 = far6[leaf // 4, f]
        n7 = far7[leaf // 8, f]
        sent[f] = buf5[(1 - core) * n5 + core * ((n5 % 8) * 8 + n5 // 8)]
        sent[8 + f] = buf6[(1 - core) * n6 + core * ((n6 % 4) * 8 + n6 // 4)]
        sent[16 + f] = buf7[(1 - core) * n7 + core * ((n7 % 2) * 8 + n7 // 2)]
    swap = send(sent, chosen.at[core], swap_send, swap_recv, to(sibling))
    chosen[core] = sent[...]
    swap.wait_recv()
    for copy in side_copies + list_copies:
        copy.wait_recv()
    for copy in map_copies + list_copies + root_copies + side_copies + [swap]:
        copy.wait_send()


def extra_rows(coords, target):
    wide = coords.astype(F32)
    norm = jnp.sum(wide * wide, axis=0, keepdims=True)
    high = norm.astype(BF16).astype(F32)
    rest = norm - high
    middle = rest.astype(BF16).astype(F32)
    low = (rest - middle).astype(BF16).astype(F32)
    shape = (16, coords.shape[1])
    row = lax.broadcasted_iota(jnp.int32, shape, 0)
    at, ones = (3, 0) if target else (0, 3)
    out = jnp.where((row >= ones) & (row < ones + 3), 1.0, 0.0)
    for n, part in enumerate((high, middle, low)):
        out = jnp.where(row == at + n, jnp.broadcast_to(part, shape), out)
    return out


def turned(coords):
    width = coords.shape[1]
    rows = [-2.0 * coords.astype(F32), extra_rows(coords, True), jnp.zeros((80, width), F32)]
    return jnp.concatenate(rows, axis=0).T.astype(BF16)


def field_kernel(
    points, charges, side_points, side_charges, nodes, side_nodes, all5, all6, all7,
    own_upper, chosen, inner_maps, leaf_maps, near_all, far_inner,
    out,
    leaf_block, node_block, leaf_turned, node_turned, near_sum, far_sum, source, owner, table,
):
    leaf = lax.axis_index("leaf")
    plane = lax.axis_index("list")
    g = leaf % 8

    def list_pair(t, count):
        i = t // 8
        slot = 4 * (t % 8) + (plane + i) % 4
        entry = near_all[(slot // 8) * 16 + i, slot % 8]
        source[count] = entry - (leaf - 1) * 16
        owner[count] = i
        return count + jnp.where(entry >= 0, 1, 0)

    live = lax.fori_loop(0, 128, list_pair, 0)
    for u in range(UNROLL):
        source[live + u] = 48
        owner[live + u] = 0

    for level in range(5):
        per = 16 >> level

        def list_far(t, carry, level=level, per=per):
            i = OFFSETS[level] + t // 8
            rel = far_inner[i, t % 8] - (leaf - 1) * per
            table[i * 8 + t % 8] = (rel // per) * NODES + OFFSETS[level] + rel % per
            return carry

        lax.fori_loop(0, per * 8, list_far, 0)
    for level in range(3):
        for f in range(8):
            table[(NODES + level) * 8 + f] = 3 * NODES + level * 8 + f

    def pack(dst, at, coords, loads):
        dst[at, 0:32] = coords
        dst[at, 32:48] = extra_rows(coords, False).astype(BF16)
        dst[at, 48:80] = loads

    for tree, (p, c) in enumerate(
        ((side_points.at[0], side_charges.at[0]), (points, charges), (side_points.at[1], side_charges.at[1]))
    ):
        for i in range(16):
            cols = slice(i * 256, (i + 1) * 256)
            pack(leaf_block, tree * 16 + i, p[:, cols], c[:, cols])
    leaf_block[48] = jnp.zeros((80, 256), BF16)

    for tree, ref in enumerate((side_nodes.at[0], nodes, side_nodes.at[1])):

        def pack_node(n, carry, tree=tree, ref=ref):
            value = ref[n]
            pack(node_block, tree * NODES + n, value[:32], value[32:])
            return carry

        lax.fori_loop(0, NODES, pack_node, 0)

    def pack_upper(f, carry):
        low, high = chosen[0, f], chosen[1, f]
        coords = jnp.concatenate([low[:16], high[:16]], axis=0)
        loads = jnp.concatenate([low[16:], high[16:]], axis=0)
        pack(node_block, 3 * NODES + f, coords, loads)
        return carry

    lax.fori_loop(0, 24, pack_upper, 0)

    for i in range(16):
        leaf_turned[i] = turned(points[:, i * 256 : (i + 1) * 256])

    def turn_node(n, carry):
        node_turned[n] = turned(nodes[n, :32])
        return carry

    lax.fori_loop(0, NODES, turn_node, 0)
    for level in range(3):
        node_turned[NODES + level] = turned(own_upper[level])

    near_sum[...] = jnp.zeros_like(near_sum)

    def near_step(step, carry):
        results = []
        for u in range(UNROLL):
            s = source[step * UNROLL + u]
            o = owner[step * UNROLL + u]
            coords = leaf_block[s, 0:48]
            loads = leaf_block[s, 48:80]
            parts = []
            for half in range(2):
                target = leaf_turned[o, half * 128 : (half + 1) * 128, 0:48]
                kernel = jnp.exp2(dot(target, coords) * RATE).astype(BF16)
                parts.append(dot_nt(loads, kernel))
            results.append((o, parts))
        for o, parts in results:
            for half in range(2):
                near_sum[o, :, half * 128 : (half + 1) * 128] += parts[half]
        return carry

    lax.fori_loop(0, (live + UNROLL - 1) // UNROLL, near_step, 0)

    def far_step(n, carry):
        target = node_turned[n, :, 0:48]
        total = jnp.zeros((32, 128), F32)
        for f in range(0, 8, 2):
            a, b = table[n * 8 + f], table[n * 8 + f + 1]
            coords = jnp.concatenate([node_block[a, 0:48], node_block[b, 0:48]], axis=1)
            loads = jnp.concatenate([node_block[a, 48:80], node_block[b, 48:80]], axis=1)
            kernel = jnp.exp2(dot(target, coords) * RATE).astype(BF16)
            total += dot_nt(loads, kernel)
        far_sum[n] = total
        return carry

    lax.fori_loop(0, NODES + 3, far_step, 0)

    def spread(total, mat):
        high = total.astype(BF16)
        low = (total - high.astype(F32)).astype(BF16)
        both = dot(jnp.concatenate([high, low], axis=0), mat)
        return both[:32] + both[32:]

    mat = jnp.concatenate([all7[n] for n in range(8)], axis=0)
    down = spread(far_sum[NODES + 2], mat)
    down = jnp.where((g // 4) % 2 == 1, down[:, 128:], down[:, :128])
    mat = jnp.concatenate([all6[4 * (g // 4) + n] for n in range(4)], axis=0)
    down = spread(far_sum[NODES + 1] + down, mat)
    down = jnp.where((g // 2) % 2 == 1, down[:, 128:], down[:, :128])
    mat = jnp.concatenate([all5[2 * (g // 2) + n] for n in range(2)], axis=0)
    down = spread(far_sum[NODES] + down, mat)
    down = jnp.where(g % 2 == 1, down[:, 128:], down[:, :128])
    totals = [far_sum[30] + down]
    for level in range(4, 0, -1):
        children = []
        for i, total in enumerate(totals):
            both = spread(total, inner_maps[OFFSETS[level] - 16 + i])
            for side in range(2):
                child = OFFSETS[level - 1] + 2 * i + side
                children.append(far_sum[child] + both[:, side * 128 : (side + 1) * 128])
        totals = children
    for i, total in enumerate(totals):
        value = near_sum[i] + spread(total, leaf_maps[i])
        out[i // 4, :, (i % 4) * 256 : (i % 4 + 1) * 256] = value.astype(BF16)


def sum_kernel(parts, out, arrived, send_sem, recv_sem):
    leaf = lax.axis_index("leaf")
    plane = lax.axis_index("list")
    barrier = pltpu.get_barrier_semaphore()
    others = [(plane + k) % 4 for k in range(1, 4)]
    for who in others:
        pl.semaphore_signal(barrier, inc=1, device_id=(leaf, who), device_id_type=MESH)
    pl.semaphore_wait(barrier, 3)
    copies = []
    for n, who in enumerate(others):
        copy = pltpu.make_async_remote_copy(
            src_ref=parts.at[who], dst_ref=arrived.at[n], send_sem=send_sem.at[n],
            recv_sem=recv_sem.at[n], device_id=(leaf, who), device_id_type=MESH,
        )
        copy.start()
        copies.append(copy)
    total = parts[plane].astype(F32)
    for n, copy in enumerate(copies):
        copy.wait_recv()
        total += arrived[n].astype(F32)
    out[...] = total
    for copy in copies:
        copy.wait_send()


def on_device(
    points, charges, leaf_ids, inner_ids, upper_ids_first, upper_ids_second, upper_ids_third,
    leaf_maps, inner_maps, upper_maps_first, upper_maps_second, upper_maps_third,
    near_lists, far_inner, far_upper_first, far_upper_second, far_upper_third,
):
    def shape(*dims, kind=BF16):
        return jax.ShapeDtypeStruct(dims, kind)

    dma = pltpu.SemaphoreType.DMA
    (side_points, side_charges, nodes, side_nodes, all5, all6, all7, near_all, own_upper, chosen) = pl.pallas_call(
        gather_kernel,
        out_shape=[
            shape(2, 32, 4096), shape(2, 32, 4096), shape(NODES, 64, 128), shape(2, NODES, 64, 128),
            shape(8, 64, 256), shape(8, 32, 256), shape(8, 16, 256), shape(4, 16, 8, kind=jnp.int32),
            shape(3, 32, 128), shape(2, 24, 32, 128),
        ],
        in_specs=[VMEM] * 13 + [SMEM] * 3,
        out_specs=[VMEM] * 10,
        scratch_shapes=[
            pltpu.VMEM((8, 64, 128), BF16), pltpu.VMEM((4, 64, 128), BF16), pltpu.VMEM((2, 64, 128), BF16),
            pltpu.VMEM((1, 64, 128), BF16), pltpu.VMEM((32, 128), BF16), pltpu.VMEM((32, 128), BF16),
            pltpu.VMEM((32, 128), BF16), pltpu.VMEM((24, 32, 128), BF16),
            pltpu.VMEM((64, 32, 128), BF16), pltpu.VMEM((32, 32, 128), BF16), pltpu.VMEM((16, 32, 128), BF16),
            dma((3, 8)), dma((3, 8)), dma((4,)), dma((4,)), dma((8,)), dma((8,)), dma((2, 3)), dma((2, 3)),
            dma((2, 3, 8)), dma((2, 3, 8)), dma, dma,
        ],
        compiler_params=pltpu.CompilerParams(collective_id=0, has_side_effects=True),
        name="gather_nodes",
    )(
        points, charges, leaf_ids, inner_ids, upper_ids_first, upper_ids_second, upper_ids_third,
        leaf_maps, inner_maps, upper_maps_first, upper_maps_second, upper_maps_third, near_lists,
        far_upper_first, far_upper_second, far_upper_third,
    )
    parts = pl.pallas_call(
        field_kernel,
        out_shape=shape(4, 32, 1024),
        in_specs=[VMEM] * 13 + [SMEM] * 2,
        out_specs=VMEM,
        scratch_shapes=[
            pltpu.VMEM((49, 80, 256), BF16), pltpu.VMEM((3 * NODES + 24, 80, 128), BF16),
            pltpu.VMEM((16, 256, 128), BF16), pltpu.VMEM((NODES + 3, 128, 128), BF16),
            pltpu.VMEM((16, 32, 256), F32), pltpu.VMEM((NODES + 3, 32, 128), F32),
            pltpu.SMEM((128 + UNROLL,), jnp.int32), pltpu.SMEM((128 + UNROLL,), jnp.int32),
            pltpu.SMEM(((NODES + 3) * 8,), jnp.int32),
        ],
        name="fields",
    )(
        points, charges, side_points, side_charges, nodes, side_nodes, all5, all6, all7, own_upper, chosen,
        inner_maps, leaf_maps, near_all.reshape(64, 8), far_inner,
    )
    return pl.pallas_call(
        sum_kernel,
        out_shape=shape(32, 1024, kind=F32),
        in_specs=[VMEM],
        out_specs=VMEM,
        scratch_shapes=[pltpu.VMEM((3, 32, 1024), BF16), dma((3,)), dma((3,))],
        compiler_params=pltpu.CompilerParams(collective_id=1, has_side_effects=True),
        name="sum_lists",
    )(parts)


def solution(mesh):
    placed = (
        P(None, "leaf"), P(None, "leaf"), P("leaf", None), P("leaf", None), P(), P(), P(),
        P("leaf", None, None), P("leaf", None, None), P("leaf", None), P("leaf", None), P("leaf", None),
        P("leaf", "list"), P("leaf", "list"), P(None, "list"), P(None, "list"), P(None, "list"),
    )
    return jax.shard_map(
        on_device, mesh=mesh, in_specs=placed, out_specs=P(None, ("leaf", "list")), check_vma=False
    )
```

time: 444 us -> 132 us (0.30)
  the two profiles are of different devices: /device:TPU:9 before, /device:TPU:4 now
where the time goes in v1:
time: 132 us
  Pallas kernels  126 us (95%)
  local copies, waits for them, and re-layouts  5.69 us (4%)
    pallas_call x1, Pallas kernels, on_device(): pl.pallas_call(gather_kernel, out_shape=[shape(2, 32, 4096), shape(2, 32,...  69.2 us
    pallas_call x1, Pallas kernels, on_device(): pl.pallas_call(field_kernel, out_shape=shape(4, 32, 1024), in_specs=[VMEM...  48 us
    pallas_call x1, Pallas kernels, on_device(): pl.pallas_call(sum_kernel, out_shape=shape(32, 1024, kind=F32), in_specs=...  8.84 us
    unnamed x14, local copies, waits for them, and re-layouts  5.69 us

profile of v1, /device:TPU:4, one launch (start us, length us, event | category | flops | bytes accessed | tf_op | source)
XLA Modules:
  0.0 131.7 jit_solution(8782118156840758118)
XLA Ops:
  0.0 0.0 copy-start
  0.0 1.4 %copy.18.near = s32[16,8]{1,0:T(8,128)} copy(s32[16,8]{0,1:T(8,128)} %param.29) | data formatting | bytes 1024 | tf_op args[12]
  1.4 0.0 copy-done
  1.4 0.0 copy-start.1
  1.4 0.7 copy.21.far7
  2.0 0.0 copy-done.1
  2.1 0.0 copy-start.2
  2.1 0.7 copy.22.far_inner
  2.7 0.0 copy-done.2
  2.7 0.0 copy-start.3
  2.7 0.7 copy.20.far6
  3.4 0.0 copy-done.3
  3.4 0.7 copy.19.far5
  4.1 69.2 %gather_nodes.1 = (bf16[2,32,4096]{2,1,0:T(8,128)(2,1)}, bf16[2,32,4096]{2,1,0:T(8,128)(2,1)}, bf16[31,64,128]{2,1,0:T(8,128)(2,1)}, bf16[2,31,64,128]{3,2,1,0:T...) custom-call(bf16[32,4096]{1,0:T(8,128)(2,1)} %points.3, ...), custom_call_target="tpu_custom_call" | custom-call | tf_op jit(solution)/shard_map/gather_nodes/pallas_call | solution.py:437
  73.3 48.0 %fields.1.parts = bf16[4,32,1024]{2,1,0:T(8,128)(2,1)} custom-call(bf16[32,4096]{1,0:T(8,128)(2,1)} %points.3, bf16[32,4096]{1,0:T(8,128)(2,1)} %charges.3, bf16[2,32,4096]{2,1,0:T(8,128)(2,1)} %get-tuple-element.15.side_points, bf16[2,32,4096]{2,1,0:T(8,128)(2,1)} %get-tuple-element.16.side_charges, bf16[31,64,128]{2,1,0:T(8,128)(2,1)} %get-tuple-element.17.nodes, ...), custom_call_target="tpu_custom_call" | custom-call | tf_op jit(solution)/shard_map/fields/pallas_call | solution.py:461
  121.3 8.8 %sum_lists.1 = f32[32,1024]{1,0:T(8,128)} custom-call(bf16[4,32,1024]{2,1,0:T(8,128)(2,1)} %fields.1.parts), custom_call_target="tpu_custom_call" | custom-call | tf_op jit(solution)/shard_map/sum_lists/pallas_call | solution.py:478
  130.2 1.6 %copy.24 = f32[32,1024]{1,0:T(8,128)} copy(f32[32,1024]{1,0:T(8,128)} %sum_lists.1) | data formatting | bytes 262144
Async XLA Ops:
  0.0 1.4 %copy-start = (s32[16,8]{0,1:T(8,128)S(1)}, s32[16,8]{0,1:T(8,128)}, u32[]{:S(2)}) copy-start(s32[16,8]{0,1:T(8,128)} %param.33) | copy-start | bytes 1540
  1.4 0.7 copy-start.1
  2.1 0.7 copy-start.2
  2.7 0.7 copy-start.3

commit v2 on v0

v2 whole, which is shorter than its diff:
```python
import math

import jax
import jax.numpy as jnp
from jax import lax
from jax.experimental import pallas as pl
from jax.experimental.pallas import tpu as pltpu
from jax.sharding import PartitionSpec as P

MESH = pl.DeviceIdType.MESH
BF16 = jnp.bfloat16
F32 = jnp.float32
VMEM = pl.BlockSpec(memory_space=pltpu.VMEM)
SMEM = pl.BlockSpec(memory_space=pltpu.SMEM)
NODES = 31
OFFSETS = (0, 16, 24, 28, 30)
RATE = -3.0 / 32.0 * math.log2(math.e)
NT = (((1,), (1,)), ((), ()))


def dot(a, b):
    return jnp.dot(a, b, preferred_element_type=F32)


def dot_nt(a, b):
    return lax.dot_general(a, b, NT, preferred_element_type=F32)


def climb(coords, weights, ids, mat):
    rows = lax.broadcasted_iota(jnp.int32, (256, 128), 0)
    hot = jnp.where(rows == ids, 1.0, 0.0).astype(BF16)
    return dot(coords, hot).astype(BF16), dot_nt(weights, mat).astype(BF16)


def extra_rows(coords, target):
    wide = coords.astype(F32)
    norm = jnp.sum(wide * wide, axis=0, keepdims=True)
    high = norm.astype(BF16).astype(F32)
    rest = norm - high
    middle = rest.astype(BF16).astype(F32)
    low = (rest - middle).astype(BF16).astype(F32)
    shape = (16, coords.shape[1])
    row = lax.broadcasted_iota(jnp.int32, shape, 0)
    at, ones = (3, 0) if target else (0, 3)
    out = jnp.where((row >= ones) & (row < ones + 3), 1.0, 0.0)
    for n, part in enumerate((high, middle, low)):
        out = jnp.where(row == at + n, jnp.broadcast_to(part, shape), out)
    return out


def turned(coords):
    width = coords.shape[1]
    rows = [-2.0 * coords.astype(F32), extra_rows(coords, True), jnp.zeros((80, width), F32)]
    return jnp.concatenate(rows, axis=0).T.astype(BF16)


def pack(dst, at, coords, loads):
    dst[at, 0:32] = coords
    dst[at, 32:48] = extra_rows(coords, False).astype(BF16)
    dst[at, 48:80] = loads


def spread(total, mat):
    high = total.astype(BF16)
    low = (total - high.astype(F32)).astype(BF16)
    both = dot(jnp.concatenate([high, low], axis=0), mat)
    return both[:32] + both[32:]


def fields(jobs):
    totals = []
    waiting = None
    for n, (target, blocks) in enumerate(jobs):
        totals.append(None)
        for coords, loads in blocks:
            distance = dot(target, coords)
            if waiting is not None:
                at, kernel, held = waiting
                term = dot_nt(held, kernel)
                totals[at] = term if totals[at] is None else totals[at] + term
            waiting = (n, jnp.exp2(distance * RATE).astype(BF16), loads)
    at, kernel, held = waiting
    term = dot_nt(held, kernel)
    totals[at] = term if totals[at] is None else totals[at] + term
    return totals


def whole_kernel(
    points, charges, leaf_ids, inner_ids, ids5, ids6, ids7, leaf_maps, inner_maps,
    maps5, maps6, maps7, near, far_inner, far5, far6, far7,
    out,
    leaf_block, node_block, leaf_turned, node_turned, near_sum, far_sum, totals,
    all5, all6, all7, roots, group5, group6, group7, half5, half6, half7, buf5, buf6, buf7, chosen,
    parts, arrived,
    map_send, map_recv, root_send, root_recv, side_send, side_recv, spread_send, spread_recv,
    ring_send, ring_recv, swap_send, swap_recv, sum_send, sum_recv,
):
    leaf = lax.axis_index("leaf")
    plane = lax.axis_index("list")
    core = leaf % 2
    y = (leaf // 2) % 8
    z = leaf // 16
    g = leaf % 8
    quad = leaf // 8
    outer = (leaf + 127 + 2 * core) % 128
    sibling = leaf + 1 - 2 * core
    group = [quad * 8 + (g + k) % 8 for k in range(1, 8)]
    row = [z * 16 + ((y + k) % 8) * 2 + core for k in range(1, 8)]
    column = [((z + k) % 8) * 16 + y * 2 + core for k in range(1, 8)]
    planes = [(leaf, (plane + k) % 4) for k in range(1, 4)]

    def to(who):
        return (who, plane)

    barrier = pltpu.get_barrier_semaphore()
    peers = [to(w) for w in (outer, sibling, *group, *row, *column)] + planes
    for who in peers:
        pl.semaphore_signal(barrier, inc=1, device_id=who, device_id_type=MESH)

    for i in range(16):
        cols = slice(i * 256, (i + 1) * 256)
        pack(leaf_block, 16 + i, points[:, cols], charges[:, cols])
    leaf_block[48] = jnp.zeros((80, 256), BF16)

    pl.semaphore_wait(barrier, len(peers))

    def remote(src, dst, s_sem, r_sem, who):
        return pltpu.make_async_remote_copy(
            src_ref=src, dst_ref=dst, send_sem=s_sem, recv_sem=r_sem, device_id=who, device_id_type=MESH
        )

    def start(copies):
        for copy in copies:
            copy.start()
        return copies

    def arrive(copies):
        for copy in copies:
            copy.wait_recv()

    levels = ((maps5, all5), (maps6, all6), (maps7, all7))
    map_same = []
    for k in (2, 4, 6, 0):
        who = sibling if k == 0 else group[k - 1]
        for n, (src, dst) in enumerate(levels):
            map_same.append(remote(src, dst.at[g], map_send.at[n, k], map_recv.at[n, k], to(who)))
    start(map_same)

    def side(n, block, stride, quarter):
        own = stride
        to_sibling = remote(
            block.at[pl.ds(own, stride)], block.at[pl.ds(2 * core * stride, stride)],
            side_send.at[n, 0], side_recv.at[n, 0], to(sibling),
        )
        to_outer = remote(
            block.at[pl.ds(own + plane * quarter, quarter)],
            block.at[pl.ds(2 * (1 - core) * stride + plane * quarter, quarter)],
            side_send.at[n, 1], side_recv.at[n, 1], to(outer),
        )
        piece = block.at[pl.ds(2 * core * stride + plane * quarter, quarter)]
        to_planes = [
            remote(piece, piece, spread_send.at[n, k], spread_recv.at[n, k], planes[k]) for k in range(3)
        ]
        return to_sibling, to_outer, to_planes

    leaf_sibling, leaf_outer, leaf_planes = side(0, leaf_block, 16, 4)
    node_sibling, node_outer, node_planes = side(1, node_block, 32, 8)
    start([leaf_outer, leaf_sibling])
    all5[g] = maps5[...]
    all6[g] = maps6[...]
    all7[g] = maps7[...]

    for i in range(16):
        cols = slice(i * 256, (i + 1) * 256)
        pack(
            node_block, 32 + i,
            *climb(points[:, cols], charges[:, cols], leaf_ids[i : i + 1, :], leaf_maps[i]),
        )
    leaf_outer.wait_recv()
    start(leaf_planes)
    for level in range(1, 5):
        for i in range(16 >> level):
            child = 32 + OFFSETS[level - 1] + 2 * i
            n = OFFSETS[level] - 16 + i
            coords = jnp.concatenate([node_block[child, 0:32], node_block[child + 1, 0:32]], axis=1)
            loads = jnp.concatenate([node_block[child, 48:80], node_block[child + 1, 48:80]], axis=1)
            pack(node_block, 48 + n, *climb(coords, loads, inner_ids[n : n + 1, :], inner_maps[n]))
    node_block[63] = jnp.zeros((80, 128), BF16)
    roots[g, :32] = node_block[62, 0:32]
    roots[g, 32:] = node_block[62, 48:80]

    root_copies = start(
        [
            remote(roots.at[g], roots.at[g], root_send.at[k], root_recv.at[k], to(group[k - 1]))
            for k in range(1, 8)
        ]
    )
    start([node_outer, node_sibling])

    map_over = []
    for k in (2, 4, 6):
        for n, (_src, dst) in enumerate(levels):
            slot = dst.at[(g + 8 - k) % 8]
            map_over.append(remote(slot, slot, map_send.at[n, k - 1], map_recv.at[n, k - 1], to(sibling)))
    arrive(map_same)
    start(map_over)

    for i in range(16):
        leaf_turned[i] = turned(points[:, i * 256 : (i + 1) * 256])
    for i in range(NODES):
        node_turned[i] = turned(node_block[32 + i, 0:32])

    arrive(map_over + root_copies)

    def keep(dst, j, coords, weights):
        dst[j, :32] = coords
        dst[j, 32:] = weights

    def join(src, j):
        both = jnp.concatenate([src[2 * j], src[2 * j + 1]], axis=1)
        return both[:32], both[32:]

    for j in range(4):
        mat = jnp.concatenate([all5[2 * j], all5[2 * j + 1]], axis=0)
        keep(group5, j, *climb(*join(roots, j), ids5[pl.ds(quad * 4 + j, 1), :], mat))
    for j in range(2):
        mat = jnp.concatenate([all6[4 * j + n] for n in range(4)], axis=0)
        keep(group6, j, *climb(*join(group5, j), ids6[pl.ds(quad * 2 + j, 1), :], mat))
    mat = jnp.concatenate([all7[n] for n in range(8)], axis=0)
    keep(group7, 0, *climb(*join(group6, 0), ids7[pl.ds(quad, 1), :], mat))

    mine = (group5[g // 2], group6[g // 4], group7[0])
    halves = (half5, half6, half7)
    bufs = (buf5, buf6, buf7)
    some = (range(1, 8), (2, 4, 6), (4,))
    every = (range(1, 8),) * 3

    def ring(c, stages):
        if c == 0:
            slots = (leaf // 2, leaf // 4, leaf // 8)
            slabs = [bufs[n].at[pl.ds(z * (8 >> n), 8 >> n)] for n in range(3)]
            plan = ((some, row), (every, column))
        else:
            slots = (y * 8 + z, (y // 2) * 8 + z, (y // 4) * 8 + z)
            slabs = [bufs[n].at[pl.ds((y // (1 << n)) * 8, 8)] for n in range(3)]
            plan = ((every, column), (some, row))
        ways = []
        for stage in range(stages):
            steps, line = plan[stage]
            ways.append(
                [
                    [
                        remote(
                            slabs[n] if stage else halves[n], slabs[n] if stage else bufs[n].at[slots[n]],
                            ring_send.at[stage, n, k], ring_recv.at[stage, n, k], to(line[k - 1]),
                        )
                        for k in steps[n]
                    ]
                    for n in range(3)
                ]
            )
        return slots, ways

    def first_stage(c):
        for n in range(3):
            halves[n][:16] = mine[n][16 * c : 16 * c + 16]
            halves[n][16:] = mine[n][32 + 16 * c : 48 + 16 * c]
        slots, (first,) = ring(c, 1)
        for n in range(3):
            start(first[n])
            bufs[n][slots[n]] = halves[n][...]

    def second_stage(c):
        _, (first, second) = ring(c, 2)
        for n in range(3):
            arrive(first[n])
            start(second[n])

    def end_stage(c):
        _, (first, second) = ring(c, 2)
        for n in range(3):
            arrive(second[n])
            for copy in first[n] + second[n]:
                copy.wait_send()

    def by_core(body):
        for c in range(2):
            pl.when(core == c)(lambda c=c: body(c))

    by_core(first_stage)
    for n in range(3):
        node_turned[NODES + n] = turned(mine[n][:32])
    node_outer.wait_recv()
    start(node_planes)

    def near_step(step, carry):
        jobs = []
        for a in range(4):
            i = step * 4 + a
            blocks = []
            for f in range(8):
                entry = near[f, i]
                s = jnp.where(entry >= 0, jnp.clip(entry - (leaf - 1) * 16, 0, 47), 48)
                blocks.append((leaf_block[s, 0:48], leaf_block[s, 48:80]))
            jobs.append((leaf_turned[i, :, 0:48], blocks))
        for a, total in enumerate(fields(jobs)):
            near_sum[step * 4 + a] = total
        return carry

    arrive([leaf_sibling] + leaf_planes)
    lax.fori_loop(0, 2, near_step, 0)
    by_core(second_stage)
    lax.fori_loop(2, 4, near_step, 0)

    def far_job(i, index):
        blocks = []
        for f in range(0, 8, 4):
            at = [index(f + n) for n in range(4)]
            blocks.append(
                (
                    jnp.concatenate([node_block[a, 0:48] for a in at], axis=1),
                    jnp.concatenate([node_block[a, 48:80] for a in at], axis=1),
                )
            )
        return node_turned[i, :, 0:48], blocks

    def inner_job(level, i):
        per = 16 >> level

        def index(f):
            rel = jnp.clip(far_inner[f, OFFSETS[level] + i] - (leaf - 1) * per, 0, 3 * per - 1)
            return (rel // per) * 32 + OFFSETS[level] + rel % per

        return far_job(OFFSETS[level] + i, index)

    arrive([node_sibling] + node_planes)
    for level in range(3):

        def far_step(step, carry, level=level):
            jobs = [inner_job(level, step * 4 + a) for a in range(4)]
            for a, total in enumerate(fields(jobs)):
                far_sum[OFFSETS[level] + step * 4 + a] = total
            return carry

        lax.fori_loop(0, 4 >> level, far_step, 0)
    for n, total in enumerate(fields([inner_job(3, 0), inner_job(3, 1), inner_job(4, 0)])):
        far_sum[28 + n] = total

    by_core(end_stage)
    for f in range(8):
        n5 = jnp.clip(far5[f, leaf // 2], 0, 63)
        n6 = jnp.clip(far6[f, leaf // 4], 0, 31)
        n7 = jnp.clip(far7[f, leaf // 8], 0, 15)
        chosen[core, f] = buf5[(1 - core) * n5 + core * ((n5 % 8) * 8 + n5 // 8)]
        chosen[core, 8 + f] = buf6[(1 - core) * n6 + core * ((n6 % 4) * 8 + n6 // 4)]
        chosen[core, 16 + f] = buf7[(1 - core) * n7 + core * ((n7 % 2) * 8 + n7 // 2)]
    swap = remote(chosen.at[core], chosen.at[core], swap_send, swap_recv, to(sibling))
    swap.start()
    swap.wait_recv()
    for f in range(24):
        low, high = chosen[0, f], chosen[1, f]
        coords = jnp.concatenate([low[:16], high[:16]], axis=0)
        pack(node_block, 96 + f, coords, jnp.concatenate([low[16:], high[16:]], axis=0))
    upper = fields([far_job(NODES + n, lambda f, n=n: 96 + n * 8 + f) for n in range(3)])

    def half_of(value, bit):
        return jnp.where(bit % 2 == 1, value[:, 128:], value[:, :128])

    mat = jnp.concatenate([all7[n] for n in range(8)], axis=0)
    down = half_of(spread(upper[2], mat), g // 4)
    mat = jnp.concatenate([all6[4 * (g // 4) + n] for n in range(4)], axis=0)
    down = half_of(spread(upper[1] + down, mat), g // 2)
    mat = jnp.concatenate([all5[2 * (g // 2) + n] for n in range(2)], axis=0)
    down = half_of(spread(upper[0] + down, mat), g)
    here = [far_sum[30] + down]
    for level in range(4, 0, -1):
        children = []
        for i, total in enumerate(here):
            both = spread(total, inner_maps[OFFSETS[level] - 16 + i])
            for n in range(2):
                child = OFFSETS[level - 1] + 2 * i + n
                children.append(far_sum[child] + both[:, n * 128 : (n + 1) * 128])
        here = children
    for i in range(16):
        totals[i] = here[i]

    sums = []
    for k in (2, 1, 3, 0):
        quarter = (plane + k) % 4
        for j in range(4):
            i = quarter * 4 + j
            value = near_sum[i] + spread(totals[i], leaf_maps[i])
            if k == 0:
                out[:, j * 256 : (j + 1) * 256] = value
            else:
                parts[k - 1, :, j * 256 : (j + 1) * 256] = value.astype(BF16)
        if k:
            sums += start(
                [remote(parts.at[k - 1], arrived.at[k - 1], sum_send.at[k], sum_recv.at[k], planes[k - 1])]
            )
    arrive(sums)
    out[...] += arrived[0].astype(F32) + arrived[1].astype(F32) + arrived[2].astype(F32)
    ended = map_same + map_over + root_copies + leaf_planes + node_planes + sums
    for copy in ended + [leaf_sibling, leaf_outer, node_sibling, node_outer, swap]:
        copy.wait_send()


def on_device(
    points, charges, leaf_ids, inner_ids, upper_ids_first, upper_ids_second, upper_ids_third,
    leaf_maps, inner_maps, upper_maps_first, upper_maps_second, upper_maps_third,
    near_lists, far_inner, far_upper_first, far_upper_second, far_upper_third,
):
    dma = pltpu.SemaphoreType.DMA

    def room(*dims, kind=BF16):
        return pltpu.VMEM(dims, kind)

    return pl.pallas_call(
        whole_kernel,
        out_shape=jax.ShapeDtypeStruct((32, 1024), F32),
        in_specs=[VMEM] * 12 + [SMEM] * 5,
        out_specs=VMEM,
        scratch_shapes=[
            room(49, 80, 256), room(96 + 24, 80, 128), room(16, 256, 128), room(NODES + 3, 128, 128),
            room(16, 32, 256, kind=F32), room(NODES, 32, 128, kind=F32), room(16, 32, 128, kind=F32),
            room(8, 64, 256), room(8, 32, 256), room(8, 16, 256),
            room(8, 64, 128), room(4, 64, 128), room(2, 64, 128), room(1, 64, 128),
            room(32, 128), room(32, 128), room(32, 128),
            room(64, 32, 128), room(32, 32, 128), room(16, 32, 128), room(2, 24, 32, 128),
            room(3, 32, 1024), room(3, 32, 1024),
            dma((3, 8)), dma((3, 8)), dma((8,)), dma((8,)), dma((2, 2)), dma((2, 2)), dma((2, 3)), dma((2, 3)),
            dma((2, 3, 8)), dma((2, 3, 8)), dma, dma, dma((4,)), dma((4,)),
        ],
        compiler_params=pltpu.CompilerParams(collective_id=0, has_side_effects=True),
        name="tree_product",
    )(
        points, charges, leaf_ids, inner_ids, upper_ids_first, upper_ids_second, upper_ids_third,
        leaf_maps, inner_maps, upper_maps_first, upper_maps_second, upper_maps_third,
        near_lists.T, far_inner.T, far_upper_first.T, far_upper_second.T, far_upper_third.T,
    )


def solution(mesh):
    placed = (
        P(None, "leaf"), P(None, "leaf"), P("leaf", None), P("leaf", None), P(), P(), P(),
        P("leaf", None, None), P("leaf", None, None), P("leaf", None), P("leaf", None), P("leaf", None),
        P("leaf", "list"), P("leaf", "list"), P(None, "list"), P(None, "list"), P(None, "list"),
    )
    return jax.shard_map(
        on_device, mesh=mesh, in_specs=placed, out_specs=P(None, ("leaf", "list")), check_vma=False
    )
```

time: 444 us -> 63.7 us (0.14)
  local copies, waits for them, and re-layouts: 115 us -> 1.57 us
  blocking collectives: 110 us -> 0 us
  Pallas kernels: 0 us -> 61.9 us
  waiting for transfers between devices: 61.6 us -> 0 us
  other arithmetic: 49.7 us -> 0 us
  starting transfers between devices: 48.3 us -> 0 us
  matrix products: 38.2 us -> 0 us
  between operations: 15.5 us -> 0.01 us
    all_gather x2 -> x0, blocking collectives: 98.1 us -> none  [on_device(): everything = lax.all_gather(shares[-1], 'leaf', axis=1, tiled=True)]
    gather x39 -> x0, local copies, waits for them, and re-layouts: 83.9 us -> none  [the longest x8 27.2 us: on_device(): jnp.take_along_axis(paired[:, :coord_dim], chosen[:, None, :], axis=2)]
    pallas_call x0 -> x1, Pallas kernels: none -> 61.9 us  [on_device(): pl.pallas_call(whole_kernel, out_shape=jax.ShapeDtypeStruct((32, 1024), F...]
    all_gather x2 -> x0, waiting for transfers between devices: 55.3 us -> none  [on_device(): everything = lax.all_gather(shares[-1], 'leaf', axis=1, tiled=True)]
    ppermute x16 -> x0, starting transfers between devices: 48.3 us -> none  [the longest x6 18.9 us: partner(): return lax.ppermute(value, axis, pairs)]
    dot_general x53 -> x0, matrix products: 38.2 us -> none  [the longest x7 12.7 us: near_round(): jnp.einsum('rpb,pab->pra', sources[coord_dim:], kernel, preferred_element...]
    and x30 -> x0, other arithmetic: 13.7 us -> none  [the longest x7 5.15 us: near_round(): targets = jnp.take(own_points, block_owners, axis=1)]
    all_to_all x1 -> x0, blocking collectives: 12.4 us -> none  [sum_at_owner(): lax.all_to_all(in_blocks(array, dim, peers), axis, 0, 0, tiled=True)]
  transfers between devices with their start and end apart: 18 -> 0, of which waited for: 7 -> 0; matrix products, arithmetic and copies ran while one was open for 38% -> 0% of each run, Pallas kernels for 0% -> 0%
where the time goes in v2:
time: 63.7 us; the launch traced here: 63.5 us
  Pallas kernels  61.9 us (97%)
  local copies, waits for them, and re-layouts  1.57 us (2%)
    pallas_call x1, Pallas kernels, on_device(): pl.pallas_call(whole_kernel, out_shape=jax.ShapeDtypeStruct((32, 1024), F...  61.9 us
    unnamed x1, local copies, waits for them, and re-layouts  1.57 us

profile of v2, /device:TPU:9, one launch (start us, length us, event | category | flops | bytes accessed | tf_op | source)
XLA Modules:
  0.0 63.5 jit_solution(18167900871947305304)
XLA Ops:
  0.0 61.9 %tree_product.1 = f32[32,1024]{1,0:T(8,128)} custom-call(bf16[32,4096]{1,0:T(8,128)(2,1)} %points.1, bf16[32,4096]{1,0:T(8,128)(2,1)} %charges.1, s32[16,128]{1,0:T(8,128)} %leaf_ids.1, s32[15,128]{1,0:T(8,128)} %inner_ids.1, s32[64,128]{1,0:T(8,128)} %ids5.1, s32[32,128]{1,0:T(8,128)} %ids6.1, s32[16,128]{1,0:T(8,128)} %ids7.1, ...), custom_call_target="tpu_custom_call" | custom-call | tf_op jit(solution)/shard_map/tree_product/pallas_call | solution.py:418
  61.9 1.6 %copy.19 = f32[32,1024]{1,0:T(8,128)} copy(f32[32,1024]{1,0:T(8,128)} %tree_product.1) | data formatting | bytes 262144

commit v3 on v2

--- a/solution.py
+++ b/solution.py
@@ -49,8 +49,7 @@
 
 
 def turned(coords):
-    width = coords.shape[1]
-    rows = [-2.0 * coords.astype(F32), extra_rows(coords, True), jnp.zeros((80, width), F32)]
+    rows = [-2.0 * coords.astype(F32), extra_rows(coords, True)]
     return jnp.concatenate(rows, axis=0).T.astype(BF16)
 
 
@@ -86,15 +85,21 @@
 
 
 def whole_kernel(
-    points, charges, leaf_ids, inner_ids, ids5, ids6, ids7, leaf_maps, inner_maps,
+    points, charges, leaf_ids, inner_ids, ids5, ids6, ids7, leaf_maps_far, inner_maps_far,
     maps5, maps6, maps7, near, far_inner, far5, far6, far7,
     out,
     leaf_block, node_block, leaf_turned, node_turned, near_sum, far_sum, totals,
     all5, all6, all7, roots, group5, group6, group7, half5, half6, half7, buf5, buf6, buf7, chosen,
-    parts, arrived,
+    parts, arrived, leaf_maps, inner_maps, fetched,
     map_send, map_recv, root_send, root_recv, side_send, side_recv, spread_send, spread_recv,
     ring_send, ring_recv, swap_send, swap_recv, sum_send, sum_recv,
 ):
+    fetches = [
+        pltpu.make_async_copy(leaf_maps_far, leaf_maps, fetched.at[0]),
+        pltpu.make_async_copy(inner_maps_far, inner_maps, fetched.at[1]),
+    ]
+    for fetch in fetches:
+        fetch.start()
     leaf = lax.axis_index("leaf")
     plane = lax.axis_index("list")
     core = leaf % 2
@@ -117,11 +122,6 @@
     for who in peers:
         pl.semaphore_signal(barrier, inc=1, device_id=who, device_id_type=MESH)
 
-    for i in range(16):
-        cols = slice(i * 256, (i + 1) * 256)
-        pack(leaf_block, 16 + i, points[:, cols], charges[:, cols])
-    leaf_block[48] = jnp.zeros((80, 256), BF16)
-
     pl.semaphore_wait(barrier, len(peers))
 
     def remote(src, dst, s_sem, r_sem, who):
@@ -152,32 +152,41 @@
             block.at[pl.ds(own, stride)], block.at[pl.ds(2 * core * stride, stride)],
             side_send.at[n, 0], side_recv.at[n, 0], to(sibling),
         )
-        to_outer = remote(
-            block.at[pl.ds(own + plane * quarter, quarter)],
-            block.at[pl.ds(2 * (1 - core) * stride + plane * quarter, quarter)],
-            side_send.at[n, 1], side_recv.at[n, 1], to(outer),
-        )
+        to_outer = []
+        for k in range(2):
+            at = ((plane + 2 * k) % 4) * quarter
+            to_outer.append(
+                remote(
+                    block.at[pl.ds(own + at, quarter)],
+                    block.at[pl.ds(2 * (1 - core) * stride + at, quarter)],
+                    side_send.at[n, 1 + k], side_recv.at[n, 1 + k], to(outer),
+                )
+            )
         piece = block.at[pl.ds(2 * core * stride + plane * quarter, quarter)]
         to_planes = [
-            remote(piece, piece, spread_send.at[n, k], spread_recv.at[n, k], planes[k]) for k in range(3)
+            remote(piece, piece, spread_send.at[n, k], spread_recv.at[n, k], planes[2 * k]) for k in range(2)
         ]
         return to_sibling, to_outer, to_planes
 
     leaf_sibling, leaf_outer, leaf_planes = side(0, leaf_block, 16, 4)
     node_sibling, node_outer, node_planes = side(1, node_block, 32, 8)
-    start([leaf_outer, leaf_sibling])
+    for i in range(16):
+        cols = slice(i * 256, (i + 1) * 256)
+        pack(leaf_block, 16 + i, points[:, cols], charges[:, cols])
+    leaf_block[48] = jnp.zeros((80, 256), BF16)
+    start(leaf_outer + [leaf_sibling])
     all5[g] = maps5[...]
     all6[g] = maps6[...]
     all7[g] = maps7[...]
 
+    fetches[0].wait()
     for i in range(16):
         cols = slice(i * 256, (i + 1) * 256)
         pack(
             node_block, 32 + i,
             *climb(points[:, cols], charges[:, cols], leaf_ids[i : i + 1, :], leaf_maps[i]),
         )
-    leaf_outer.wait_recv()
-    start(leaf_planes)
+    fetches[1].wait()
     for level in range(1, 5):
         for i in range(16 >> level):
             child = 32 + OFFSETS[level - 1] + 2 * i
@@ -195,7 +204,7 @@
             for k in range(1, 8)
         ]
     )
-    start([node_outer, node_sibling])
+    start(node_outer + [node_sibling])
 
     map_over = []
     for k in (2, 4, 6):
@@ -206,9 +215,9 @@
     start(map_over)
 
     for i in range(16):
-        leaf_turned[i] = turned(points[:, i * 256 : (i + 1) * 256])
-    for i in range(NODES):
-        node_turned[i] = turned(node_block[32 + i, 0:32])
+        leaf_turned[i, :, 0:48] = turned(points[:, i * 256 : (i + 1) * 256])
+    leaf_outer[0].wait_recv()
+    start(leaf_planes)
 
     arrive(map_over + root_copies)
 
@@ -280,6 +289,10 @@
         _, (first, second) = ring(c, 2)
         for n in range(3):
             arrive(second[n])
+
+    def end_sends(c):
+        _, (first, second) = ring(c, 2)
+        for n in range(3):
             for copy in first[n] + second[n]:
                 copy.wait_send()
 
@@ -289,8 +302,10 @@
 
     by_core(first_stage)
     for n in range(3):
-        node_turned[NODES + n] = turned(mine[n][:32])
-    node_outer.wait_recv()
+        node_turned[NODES + n, :, 0:48] = turned(mine[n][:32])
+    for i in range(NODES):
+        node_turned[i, :, 0:48] = turned(node_block[32 + i, 0:32])
+    node_outer[0].wait_recv()
     start(node_planes)
 
     def near_step(step, carry):
@@ -307,7 +322,7 @@
             near_sum[step * 4 + a] = total
         return carry
 
-    arrive([leaf_sibling] + leaf_planes)
+    arrive([leaf_sibling, leaf_outer[1]] + leaf_planes)
     lax.fori_loop(0, 2, near_step, 0)
     by_core(second_stage)
     lax.fori_loop(2, 4, near_step, 0)
@@ -333,8 +348,8 @@
 
         return far_job(OFFSETS[level] + i, index)
 
-    arrive([node_sibling] + node_planes)
-    for level in range(3):
+    arrive([node_sibling, node_outer[1]] + node_planes)
+    for level in range(1):
 
         def far_step(step, carry, level=level):
             jobs = [inner_job(level, step * 4 + a) for a in range(4)]
@@ -343,9 +358,6 @@
             return carry
 
         lax.fori_loop(0, 4 >> level, far_step, 0)
-    for n, total in enumerate(fields([inner_job(3, 0), inner_job(3, 1), inner_job(4, 0)])):
-        far_sum[28 + n] = total
-
     by_core(end_stage)
     for f in range(8):
         n5 = jnp.clip(far5[f, leaf // 2], 0, 63)
@@ -356,6 +368,18 @@
         chosen[core, 16 + f] = buf7[(1 - core) * n7 + core * ((n7 % 2) * 8 + n7 // 2)]
     swap = remote(chosen.at[core], chosen.at[core], swap_send, swap_recv, to(sibling))
     swap.start()
+    for level in range(1, 3):
+
+        def far_step(step, carry, level=level):
+            jobs = [inner_job(level, step * 4 + a) for a in range(4)]
+            for a, total in enumerate(fields(jobs)):
+                far_sum[OFFSETS[level] + step * 4 + a] = total
+            return carry
+
+        lax.fori_loop(0, 4 >> level, far_step, 0)
+    for n, total in enumerate(fields([inner_job(3, 0), inner_job(3, 1), inner_job(4, 0)])):
+        far_sum[28 + n] = total
+
     swap.wait_recv()
     for f in range(24):
         low, high = chosen[0, f], chosen[1, f]
@@ -401,8 +425,9 @@
     arrive(sums)
     out[...] += arrived[0].astype(F32) + arrived[1].astype(F32) + arrived[2].astype(F32)
     ended = map_same + map_over + root_copies + leaf_planes + node_planes + sums
-    for copy in ended + [leaf_sibling, leaf_outer, node_sibling, node_outer, swap]:
+    for copy in ended + leaf_outer + node_outer + [leaf_sibling, node_sibling, swap]:
         copy.wait_send()
+    by_core(end_sends)
 
 
 def on_device(
@@ -418,7 +443,7 @@
     return pl.pallas_call(
         whole_kernel,
         out_shape=jax.ShapeDtypeStruct((32, 1024), F32),
-        in_specs=[VMEM] * 12 + [SMEM] * 5,
+        in_specs=[VMEM] * 7 + [pl.BlockSpec(memory_space=pl.ANY)] * 2 + [VMEM] * 3 + [SMEM] * 5,
         out_specs=VMEM,
         scratch_shapes=[
             room(49, 80, 256), room(96 + 24, 80, 128), room(16, 256, 128), room(NODES + 3, 128, 128),
@@ -427,8 +452,8 @@
             room(8, 64, 128), room(4, 64, 128), room(2, 64, 128), room(1, 64, 128),
             room(32, 128), room(32, 128), room(32, 128),
             room(64, 32, 128), room(32, 32, 128), room(16, 32, 128), room(2, 24, 32, 128),
-            room(3, 32, 1024), room(3, 32, 1024),
-            dma((3, 8)), dma((3, 8)), dma((8,)), dma((8,)), dma((2, 2)), dma((2, 2)), dma((2, 3)), dma((2, 3)),
+            room(3, 32, 1024), room(3, 32, 1024), room(16, 128, 256), room(15, 128, 256), dma((2,)),
+            dma((3, 8)), dma((3, 8)), dma((8,)), dma((8,)), dma((2, 3)), dma((2, 3)), dma((2, 2)), dma((2, 2)),
             dma((2, 3, 8)), dma((2, 3, 8)), dma, dma, dma((4,)), dma((4,)),
         ],
         compiler_params=pltpu.CompilerParams(collective_id=0, has_side_effects=True),

time: 63.7 us -> 61.8 us (0.970)
  Pallas kernels: 61.9 us -> 60.1 us
    pallas_call x1, Pallas kernels: 61.9 us -> 60.1 us  [on_device(): pl.pallas_call(whole_kernel, out_shape=jax.ShapeDtypeStruct((32, 1024), F...]
where the time goes in v3:
time: 61.8 us; the launch traced here: 61.7 us
  Pallas kernels  60.1 us (97%)
  local copies, waits for them, and re-layouts  1.57 us (3%)
    pallas_call x1, Pallas kernels, on_device(): pl.pallas_call(whole_kernel, out_shape=jax.ShapeDtypeStruct((32, 1024), F...  60.1 us
    unnamed x1, local copies, waits for them, and re-layouts  1.57 us

profile of v3, /device:TPU:9, one launch (start us, length us, event | category | flops | bytes accessed | tf_op | source)
XLA Modules:
  0.0 61.7 jit_solution(5281682036614753058)
XLA Ops:
  0.0 60.1 %tree_product.1 = f32[32,1024]{1,0:T(8,128)} custom-call(bf16[32,4096]{1,0:T(8,128)(2,1)} %points.1, bf16[32,4096]{1,0:T(8,128)(2,1)} %charges.1, s32[16,128]{1,0:T(8,128)} %leaf_ids.1, s32[15,128]{1,0:T(8,128)} %inner_ids.1, s32[64,128]{1,0:T(8,128)} %ids5.1, s32[32,128]{1,0:T(8,128)} %ids6.1, s32[16,128]{1,0:T(8,128)} %ids7.1, ...), custom_call_target="tpu_custom_call" | custom-call | tf_op jit(solution)/shard_map/tree_product/pallas_call | solution.py:443
  60.1 1.6 %copy.19 = f32[32,1024]{1,0:T(8,128)} copy(f32[32,1024]{1,0:T(8,128)} %tree_product.1) | data formatting | bytes 262144
